TPU v7x, 256 devices: a whole 4x4x8 slice. The times are simulated.
256 devices in a mesh: pair: 64 (over x, z, core), aux: 4 (over y).
Axes of the slice: x: 4, y: 4, z: 8, core: 2. Of those that a mesh axis runs over, the one named last changes fastest.
Arguments:
- factor: float32 [131072, 4096], P('pair', 'aux'), may hold values from -0.015625 to 0.015625
- trials: float32 [256, 131072], P('aux', 'pair'), may hold values from -6 to 6
- stored: float32 [384, 131072], P(None, 'pair'), may hold values from -0.015625 to 0.015625
- energy_gaps: float32 [131072], P('pair'), may hold values from 0.35 to 7
Outputs:
- next_trials: float32 [256, 131072], P('aux', 'pair')
- projections: float32 [2, 384, 256], P(None, None, 'aux')
All inputs are finite; a program needn't handle non-finite values.
Results may differ from a plain program's by a relative error of at most 0.0001.
Values sent between devices are 32-bit elements; how exact they have to be, the bound alone decides.
A program may use at most 64 MiB of HBM per device.

v0:
```python
import math

import jax
import jax.numpy as jnp
from jax import lax
from jax.sharding import Mesh
from jax.sharding import PartitionSpec as P

PAIRS = 131072
ROUNDS = 2
PAIR = ("pair_0", "pair_1", "pair_2")


def side_by_side(arrays, axis, dim, along):
    widths = [math.prod(a.shape[along:]) for a in arrays]
    both = jnp.concatenate(
        [a.reshape(*a.shape[:along], w) for a, w in zip(arrays, widths)], axis=along
    )
    whole = lax.all_gather(both, axis, axis=dim, tiled=True)
    blocks = jnp.split(whole, [sum(widths[:k]) for k in range(1, len(widths))], axis=along)
    return tuple(
        (b.reshape(*whole.shape[:along], *a.shape[along:]) for a, b in zip(arrays, blocks))
    )


def split_up(x, dim, count):
    before, after = (x.shape[:dim], x.shape[dim + 1 :])
    return jnp.moveaxis(x.reshape(*before, count, -1, *after), dim, 0)


def sum_at_owner(x, axis, dim):
    blocks = split_up(x, dim, lax.axis_size(axis))
    arrived = lax.all_to_all(blocks, axis, split_axis=0, concat_axis=0, tiled=True)
    return arrived.sum(axis=0)


def sum_by_axis(x, axes, dim):
    far, near = axes
    own = sum_at_owner(split_up(x, dim, lax.axis_size(far)), near, dim + 1)
    return jnp.sum(lax.all_to_all(own, far, 0, 0, tiled=True), axis=0)


def rows_for(lines, count):
    spare = -len(lines) % count
    return jnp.pad(lines, [(0, spare)] + [(0, 0)] * (lines.ndim - 1))


def sent_to_all(x, axis):
    count = lax.axis_size(axis)
    return lax.all_to_all(jnp.broadcast_to(x[None], (count, *x.shape)), axis, 0, 0, tiled=True)


def laid_out(blocks, dim):
    blocks = jnp.moveaxis(blocks, 0, dim)
    dims = blocks.shape
    return blocks.reshape(*dims[:dim], dims[dim] * dims[dim + 1], *dims[dim + 2 :])


def whole_of(x, axes, dim):
    far, near = axes
    leading = sent_to_all(x, far)
    blocks = jnp.swapaxes(sent_to_all(leading, near), 0, 1)
    return laid_out(blocks.reshape(-1, *x.shape), dim)


def nested_sum(x, axes):
    lines = x.reshape(-1, x.shape[-1])
    own = sum_by_axis(rows_for(lines, lax.axis_size(axes[0]) * lax.axis_size(axes[1])), axes, 0)
    whole = whole_of(own, axes, 0)
    return whole[: len(lines)].reshape(x.shape)


def gather_directly(x, axis, dim):
    return laid_out(sent_to_all(x, axis), dim)


def total_of(x, axes):
    lines = x.reshape(-1, x.shape[-1])
    own = sum_at_owner(rows_for(lines, lax.axis_size(axes)), axes, 0)
    whole = gather_directly(own, axes, 0)
    return whole[: len(lines)].reshape(x.shape)


def taken_together(x, axis):
    return sent_to_all(x, axis).sum(axis=0)


def on_device(factor, trials, stored, energy_gaps):
    highest = lax.Precision.HIGHEST
    own_rows = trials
    row_norms = jnp.ones((trials.shape[0],), jnp.float32)
    collected = []
    for turn_index in range(ROUNDS):
        everything, every_norm = side_by_side((own_rows, row_norms), "aux", 0, 1)
        true_rows = own_rows / row_norms[:, None]
        partial_value = jnp.dot(
            everything, factor, precision=highest, preferred_element_type=jnp.float32
        )
        partial_value = partial_value / every_norm[:, None]
        fitted = nested_sum(partial_value, (("pair_0", "pair_1"), "pair_2"))
        spread = lax.dot_general(
            fitted,
            factor,
            (((1,), (1,)), ((), ())),
            precision=highest,
            preferred_element_type=jnp.float32,
        )
        own_response = sum_at_owner(4.0 * spread, "aux", 0)
        response = energy_gaps[None, :] * true_rows + own_response
        local_intersection = lax.dot_general(
            stored,
            response,
            (((1,), (1,)), ((), ())),
            precision=highest,
            preferred_element_type=jnp.float32,
        )
        projection = total_of(local_intersection, PAIR)
        removed = lax.dot_general(
            projection,
            stored,
            (((0,), (0,)), ((), ())),
            precision=highest,
            preferred_element_type=jnp.float32,
        )
        scaled = (response - removed) / energy_gaps[None, :]
        square_sum = taken_together(jnp.sum(scaled * scaled, axis=1), PAIR)
        row_norms = jnp.sqrt(square_sum / PAIRS + 1e-06)
        if turn_index + 1 < ROUNDS:
            own_rows = scaled
        else:
            own_rows = scaled / row_norms[:, None]
        collected.append(projection)
    return (own_rows, jnp.stack(collected))


def solution(mesh):
    split = Mesh(
        mesh.devices.reshape(4, 8, 2, mesh.shape["aux"]), ("pair_0", "pair_1", "pair_2", "aux")
    )
    return jax.shard_map(
        on_device,
        mesh=split,
        in_specs=(P(PAIR, "aux"), P("aux", PAIR), P(None, PAIR), P(PAIR)),
        out_specs=(P("aux", PAIR), P(None, None, "aux")),
        check_vma=False,
    )
```

profile of v0, /device:TPU:1, one launch (start us, length us, event | category | flops | bytes accessed | tf_op | source)
XLA Modules:
  0.0 466.8 jit_solution(12003833695849297342)
XLA Ops:
  7.2 2.0 concatenate.6
  9.3 38.5 %all-gather.3.cloned.1.call-done = f32[256,2049]{1,0:T(8,128)} async-done(((f32[64,2049]{1,0:T(8,128)}), f32[256,2049]{1,0:T(8,128)}) %all-gather.3.cloned.1.call-update) | async-done | bytes 2098192 | tf_op jit(solution)/shard_map/all_gather | solution.py:19
  47.9 1.0 slice_reduce_fusion.1
  48.9 11.1 %fusion.4 = f32[256,1024]{1,0:T(8,128)} fusion(f32[2048,1024]{1,0:T(8,128)} %param.4, f32[256,2049]{1,0:T(8,128)} %all-gather.3.cloned.1.call-done, f32[256]{0:T(256)S(1)} %slice_reduce_fusion.1), kind=kOutput, calls=%fused_computation.8 | convolution fusion | flops 6442713088 | bytes 11535360 | tf_op jit(solution)/shard_map/dot_general | solution.py:96
  60.0 2.5 reshape_reshape.12
  62.6 1.3 copy.44
  63.9 5.8 %all_to_all.82 = f32[2,32,4,1024]{3,2,1,0:T(4,128)} all-to-all(f32[2,32,4,1024]{3,2,1,0:T(4,128)S(1)} %bitcast.32), channel_id=1, replica_groups=mesh['pair_0'=4,'pair_1'=8,'pair_2'=2,'aux'=4] {'pair_2'}, dimensions={0} | all-to-all | bytes 2097152 | tf_op jit(solution)/shard_map/all_to_all | solution.py:33
  69.7 2.5 reduce_sum.108
  72.2 23.8 %all_to_all.83 = f32[32,4,1024]{2,1,0:T(4,128)} all-to-all(f32[32,4,1024]{2,1,0:T(4,128)} %reduce_sum.108), channel_id=1, replica_groups=mesh['pair_0'=4,'pair_1'=8,'pair_2'=2,'aux'=4] {'pair_0','pair_1'}, dimensions={0} | all-to-all | bytes 1048576 | tf_op jit(solution)/shard_map/all_to_all | solution.py:40
  96.0 1.1 reduce_sum.109
  97.2 22.4 %all_to_all.84 = f32[32,4,1024]{2,1,0:T(4,128)S(1)} all-to-all(f32[32,4,1024]{2,1,0:T(4,128)S(1)} %broadcast_in_dim.16), channel_id=1, replica_groups=mesh['pair_0'=4,'pair_1'=8,'pair_2'=2,'aux'=4] {'pair_0','pair_1'}, dimensions={0} | all-to-all | bytes 1048576 | tf_op jit(solution)/shard_map/all_to_all | solution.py:50
  119.9 7.3 %all_to_all.85 = f32[2,32,4,1024]{3,2,1,0:T(4,128)S(1)} all-to-all(f32[2,32,4,1024]{3,2,1,0:T(4,128)S(1)} %broadcast_in_dim.17), channel_id=1, replica_groups=mesh['pair_0'=4,'pair_1'=8,'pair_2'=2,'aux'=4] {'pair_2'}, dimensions={0} | all-to-all | bytes 2097152 | tf_op jit(solution)/shard_map/all_to_all | solution.py:50
  127.3 1.1 copy.29
  128.4 2.6 reshape_reshape.13
  131.0 9.9 %convolution_multiply_fusion.1 = f32[256,2048]{1,0:T(8,128)S(1)} fusion(f32[256,1024]{1,0:T(8,128)} %reshape_reshape.13, f32[2048,1024]{1,0:T(8,128)} %param.4), kind=kOutput, calls=%fused_computation.1 | convolution fusion | flops 6442975232 | bytes 11534336 | tf_op jit(solution)/shard_map/dot_general | solution.py:101
  140.9 29.4 %all_to_all.86 = f32[4,64,2048]{2,1,0:T(8,128)} all-to-all(f32[4,64,2048]{2,1,0:T(8,128)S(1)} %bitcast.30), channel_id=1, replica_groups=mesh['pair_0'=4,'pair_1'=8,'pair_2'=2,'aux'=4] {'aux'}, dimensions={0} | all-to-all | bytes 4194304 | tf_op jit(solution)/shard_map/all_to_all | solution.py:33
  170.4 2.6 reduce_sum.110
  172.9 4.1 convolution_bitcast_fusion.1
  177.0 0.8 copy.30
  177.9 1.0 reshape.67
  179.0 17.1 %all_to_all.87 = f32[64,1,384]{2,1,0:T(1,128)S(1)} all-to-all(f32[64,1,384]{2,1,0:T(1,128)S(1)} %reshape.74), channel_id=1, replica_groups=mesh['pair_0'=4,'pair_1'=8,'pair_2'=2,'aux'=4] {'pair_0','pair_1','pair_2'}, dimensions={0} | all-to-all | bytes 196608 | tf_op jit(solution)/shard_map/all_to_all | solution.py:33
  196.6 0.8 reduce.6
  197.9 14.3 %all_to_all.88 = f32[64,1,384]{2,1,0:T(1,128)S(1)} all-to-all(f32[64,1,384]{2,1,0:T(1,128)S(1)} %reshape.76), channel_id=1, replica_groups=mesh['pair_0'=4,'pair_1'=8,'pair_2'=2,'aux'=4] {'pair_0','pair_1','pair_2'}, dimensions={0} | all-to-all | bytes 196608 | tf_op jit(solution)/shard_map/all_to_all | solution.py:50
  212.2 0.8 reduce.7
  213.8 4.3 multiply_reduce_fusion.1
  218.2 13.7 %all_to_all.89 = f32[64,1,64]{2,1,0:T(1,128)S(1)} all-to-all(f32[64,1,64]{2,1,0:T(1,128)S(1)} %broadcast_in_dim.19), channel_id=1, replica_groups=mesh['pair_0'=4,'pair_1'=8,'pair_2'=2,'aux'=4] {'pair_0','pair_1','pair_2'}, dimensions={0} | all-to-all | bytes 32768 | tf_op jit(solution)/shard_map/all_to_all | solution.py:50
  232.1 1.9 pad_maximum_fusion
  234.0 27.3 %all-gather.5.cloned.1.call-done = f32[256,2049]{1,0:T(8,128)} async-done(((f32[64,2049]{1,0:T(8,128)}), f32[256,2049]{1,0:T(8,128)}) %all-gather.5.cloned.1.call-update) | async-done | bytes 2098192 | tf_op jit(solution)/shard_map/all_gather | solution.py:19
  261.3 1.0 slice_reduce_fusion
  262.3 11.1 %fusion.7 = f32[256,1024]{1,0:T(8,128)} fusion(f32[2048,1024]{1,0:T(8,128)} %param.4, f32[256,2049]{1,0:T(8,128)} %all-gather.5.cloned.1.call-done, f32[256]{0:T(256)S(1)} %slice_reduce_fusion), kind=kOutput, calls=%fused_computation.9 | convolution fusion | flops 6442713088 | bytes 11535360 | tf_op jit(solution)/shard_map/dot_general | solution.py:96
  273.5 2.5 reshape_reshape.14
  276.0 1.3 copy.43
  277.3 5.8 %all_to_all.90 = f32[2,32,4,1024]{3,2,1,0:T(4,128)} all-to-all(f32[2,32,4,1024]{3,2,1,0:T(4,128)S(1)} %bitcast.34), channel_id=1, replica_groups=mesh['pair_0'=4,'pair_1'=8,'pair_2'=2,'aux'=4] {'pair_2'}, dimensions={0} | all-to-all | bytes 2097152 | tf_op jit(solution)/shard_map/all_to_all | solution.py:33
  283.1 2.5 reduce_sum.114
  285.6 23.8 %all_to_all.91 = f32[32,4,1024]{2,1,0:T(4,128)} all-to-all(f32[32,4,1024]{2,1,0:T(4,128)} %reduce_sum.114), channel_id=1, replica_groups=mesh['pair_0'=4,'pair_1'=8,'pair_2'=2,'aux'=4] {'pair_0','pair_1'}, dimensions={0} | all-to-all | bytes 1048576 | tf_op jit(solution)/shard_map/all_to_all | solution.py:40
  309.4 1.1 reduce_sum.115
  310.7 22.4 %all_to_all.92 = f32[32,4,1024]{2,1,0:T(4,128)S(1)} all-to-all(f32[32,4,1024]{2,1,0:T(4,128)S(1)} %broadcast_in_dim.20), channel_id=1, replica_groups=mesh['pair_0'=4,'pair_1'=8,'pair_2'=2,'aux'=4] {'pair_0','pair_1'}, dimensions={0} | all-to-all | bytes 1048576 | tf_op jit(solution)/shard_map/all_to_all | solution.py:50
  333.4 7.3 %all_to_all.93 = f32[2,32,4,1024]{3,2,1,0:T(4,128)S(1)} all-to-all(f32[2,32,4,1024]{3,2,1,0:T(4,128)S(1)} %broadcast_in_dim.21), channel_id=1, replica_groups=mesh['pair_0'=4,'pair_1'=8,'pair_2'=2,'aux'=4] {'pair_2'}, dimensions={0} | all-to-all | bytes 2097152 | tf_op jit(solution)/shard_map/all_to_all | solution.py:50
  340.7 1.1 copy.35
  341.8 2.6 reshape_reshape.15
  344.4 9.9 %convolution_multiply_fusion = f32[256,2048]{1,0:T(8,128)S(1)} fusion(f32[256,1024]{1,0:T(8,128)} %reshape_reshape.15, f32[2048,1024]{1,0:T(8,128)} %param.4), kind=kOutput, calls=%fused_computation | convolution fusion | flops 6442975232 | bytes 11534336 | tf_op jit(solution)/shard_map/dot_general | solution.py:101
  354.3 29.5 %all_to_all.94 = f32[4,64,2048]{2,1,0:T(8,128)} all-to-all(f32[4,64,2048]{2,1,0:T(8,128)S(1)} %bitcast.31), channel_id=1, replica_groups=mesh['pair_0'=4,'pair_1'=8,'pair_2'=2,'aux'=4] {'aux'}, dimensions={0} | all-to-all | bytes 4194304 | tf_op jit(solution)/shard_map/all_to_all | solution.py:33
  383.9 2.6 reduce_sum.116
  386.4 4.2 convolution_bitcast_fusion
  390.6 0.8 copy.36
  391.4 1.6 reshape.70
  393.1 1.7 reshape.78
  394.8 17.3 %all_to_all.95 = f32[64,1,384]{2,1,0:T(1,128)S(1)} all-to-all(f32[64,1,384]{2,1,0:T(1,128)} %reshape.78), channel_id=1, replica_groups=mesh['pair_0'=4,'pair_1'=8,'pair_2'=2,'aux'=4] {'pair_0','pair_1','pair_2'}, dimensions={0} | all-to-all | bytes 196608 | tf_op jit(solution)/shard_map/all_to_all | solution.py:33
  412.1 1.5 reduce.8
  413.6 1.7 reshape.79
  415.3 1.0 reduce_sum.117
  416.3 0.7 broadcast_in_dim.22
  417.0 1.7 reshape.80
  418.8 4.4 all-to-all-start.14
  423.9 9.6 %all-to-all-done.14 = f32[64,1,384]{2,1,0:T(1,128)S(1)} async-done(((f32[64,1,384]{2,1,0:T(1,128)}), f32[64,1,384]{2,1,0:T(1,128)S(1)}, u32[]{:S(2)}, u32[]{:S(2)}) %all-to-all-start.14) | async-done | bytes 98336 | tf_op jit(solution)/shard_map/all_to_all | solution.py:50
  433.5 1.5 reduce.9
  435.0 1.0 reshape.81
  437.4 4.2 multiply_reduce_fusion
  442.2 5.2 %all-to-all-start.15 = ((f32[64,1,64]{2,1,0:T(1,128)}), f32[64,1,64]{2,1,0:T(1,128)}, u32[]{:S(2)}, u32[]{:S(2)}) async-start(f32[64,1,64]{2,1,0:T(1,128)} %broadcast_in_dim.23), calls=%async_computation.15 | async-start | bytes 65536 | tf_op jit(solution)/shard_map/all_to_all | solution.py:50
  447.4 1.1 pad_maximum_fusion.1
  448.5 0.8 copy.38
  449.3 7.5 %all-to-all-done.15 = f32[64,1,64]{2,1,0:T(1,128)} async-done(((f32[64,1,64]{2,1,0:T(1,128)}), f32[64,1,64]{2,1,0:T(1,128)}, u32[]{:S(2)}, u32[]{:S(2)}) %all-to-all-start.15) | async-done | bytes 16416 | tf_op jit(solution)/shard_map/all_to_all | solution.py:50
  456.8 0.8 reduce_sum.119
  457.6 2.0 multiply_divide_fusion
  (29 shorter events, 5.6 us)
Async XLA Ops:
  7.2 165.8 %copy-start = (f32[384,2048]{1,0:T(8,128)S(1)}, f32[384,2048]{1,0:T(8,128)}, u32[]{:S(2)}) copy-start(f32[384,2048]{1,0:T(8,128)} %param.6) | copy-start | bytes 9437188
  7.2 40.7 %all-gather.3.cloned.1.call-start = ((), (), s32[]{:S(2)}) async-start(), calls=%async_computation.16 | async-start | bytes 2785280 | tf_op jit(solution)/shard_map/all_gather | solution.py:19
  9.3 252.0 %all-gather.5.cloned.1.call-start = ((), (), s32[]{:S(2)}) async-start(), calls=%async_computation.17 | async-start | bytes 2785280 | tf_op jit(solution)/shard_map/all_gather | solution.py:19
  140.9 32.0 %copy-start.1 = (f32[2048]{0:T(1024)S(1)}, f32[2048]{0:T(1024)}, u32[]{:S(2)}) copy-start(f32[2048]{0:T(1024)} %param.7) | copy-start | bytes 24580
  418.8 14.7 %all-to-all-start.14 = ((f32[64,1,384]{2,1,0:T(1,128)}), f32[64,1,384]{2,1,0:T(1,128)S(1)}, u32[]{:S(2)}, u32[]{:S(2)}) async-start(f32[64,1,384]{2,1,0:T(1,128)} %reshape.80), calls=%async_computation.14 | async-start | bytes 196608 | tf_op jit(solution)/shard_map/all_to_all | solution.py:50
  442.2 14.6 %all-to-all-start.15 = ((f32[64,1,64]{2,1,0:T(1,128)}), f32[64,1,64]{2,1,0:T(1,128)}, u32[]{:S(2)}, u32[]{:S(2)}) async-start(f32[64,1,64]{2,1,0:T(1,128)} %broadcast_in_dim.23), calls=%async_computation.15 | async-start | bytes 65536 | tf_op jit(solution)/shard_map/all_to_all | solution.py:50
Sparse Core Ops, SparseCore 0:
  9.8 38.0 all-gather.2
  234.1 27.1 all-gather.4
where the time goes:
time: 476 us; the launch traced here: 467 us
  blocking collectives  240 us (50%)
  waiting for transfers between devices  82.9 us (17%)
  matrix products  59 us (12%)
  local copies, waits for them, and re-layouts  36.4 us (8%)
  other arithmetic  23.8 us (5%)
  between operations  14.7 us (3%)
  starting transfers between devices  9.74 us (2%)
    all_to_all x6, blocking collectives, sum_at_owner(): lax.all_to_all(blocks, axis, split_axis=0, concat_axis=0, tiled=True)  105 us
    all_to_all x6, blocking collectives, sent_to_all(): lax.all_to_all(jnp.broadcast_to(x[None], (count, *x.shape)), axis, 0, 0,...  87.6 us
    all_gather x2, waiting for transfers between devices, side_by_side(): whole = lax.all_gather(both, axis, axis=dim, tiled=True)  65.8 us
    all_to_all x2, blocking collectives, sum_by_axis(): return jnp.sum(lax.all_to_all(own, far, 0, 0, tiled=True), axis=0)  47.6 us
    dot_general x2, matrix products, on_device(): jnp.dot(everything, factor, precision=highest, preferred_element_type=jnp...  22.3 us
    dot_general x2, matrix products, on_device(): lax.dot_general(fitted, factor, (((1,), (1,)), ((), ())), precision=highe...  19.9 us
    all_to_all x2, waiting for transfers between devices, sent_to_all(): lax.all_to_all(jnp.broadcast_to(x[None], (count, *x.shape)), axis, 0, 0,...  17.1 us
    reduce_sum x6, other arithmetic, sum_at_owner(): return arrived.sum(axis=0)  11.1 us
  transfers between devices with their start and end apart: 4, of which 4 were waited for; matrix products, arithmetic and copies ran while one was open for 1% of the time, Pallas kernels for 0%

commit v1 on v0

v1 whole, which is shorter than its diff:
```python
import functools

import jax
import jax.numpy as jnp
from jax import lax
from jax.experimental import pallas as pl
from jax.experimental.pallas import tpu as pltpu
from jax.sharding import Mesh
from jax.sharding import PartitionSpec as P

PAIRS = 131072
ROUNDS = 2
CH = 2
MESH = pl.DeviceIdType.MESH
F32 = jnp.float32
BF16 = jnp.bfloat16
NT = (((1,), (1,)), ((), ()))
NN = (((1,), (0,)), ((), ()))


def halves(v):
    hi = v.astype(BF16)
    lo = (v - hi.astype(F32)).astype(BF16)
    return hi, lo


def dot(a, b, dims):
    return lax.dot_general(a, b, dims, preferred_element_type=F32)


def dot3(stacked, m, b_hi, b_lo, dims):
    both = dot(stacked, b_hi, dims)
    return both[:m] + both[m:] + dot(stacked[:m], b_lo, dims)


def kernel(nx, nz, total_pairs, factor, trials, stored, gaps, o_next, o_proj,
           f32v, fhi, flo, s32v, shi, slo, gapv,
           xg, xs, fp, fx, fsum, rbuf, piece, fit, fs, w, tbuf, win, resp, rs,
           pp, prx, psm, prz, pz, pfull, srx, sq1, srz, sq0,
           load_sem, ag_s, ag_r, cx_s, cx_r, pr_s, pr_r, pa_s, pa_r, cy_s, cy_r,
           ys_s, ys_r, px_s, px_r, pz_s, pz_r, py_s, py_r, qx_s, qx_r, qz_s, qz_r):
    rows, pairs = trials.shape
    aux = factor.shape[1]
    n_st = stored.shape[0]
    rc = rows // CH
    rh = rc // 2
    m = 4 * rc
    half = 2 * rc
    rb = half // nx
    cb = aux // nz
    nxz = nx * nz
    nxc = 2 * nx
    pr = rows // nxc
    x, z = lax.axis_index("x"), lax.axis_index("z")
    c, y = lax.axis_index("core"), lax.axis_index("aux")
    right, left = lax.rem(y + 1, 4), lax.rem(y + 3, 4)

    def at(x_=None, z_=None, c_=None, y_=None):
        pick = lambda v, d: d if v is None else v
        return (pick(x_, x), pick(z_, z), pick(c_, c), pick(y_, y))

    def plane(k):
        return at(x_=lax.rem(x + k // nz, nx), z_=lax.rem(z + k % nz, nz))

    def row_peer(k):
        return at(x_=lax.rem(x + k // 2, nx), c_=lax.rem(c + k % 2, 2))

    def z_peer(k):
        return at(z_=lax.rem(z + k, nz))

    def remote(src, dst, s, r, dev):
        return pltpu.make_async_remote_copy(
            src_ref=src, dst_ref=dst, send_sem=s, recv_sem=r, device_id=dev,
            device_id_type=MESH)

    def arrived(refs, sem):
        pltpu.make_async_copy(refs, refs, sem).wait()

    bar = pltpu.get_barrier_semaphore()

    def greet(dev):
        pl.semaphore_signal(bar, inc=1, device_id=dev, device_id_type=MESH)

    greet(at(y_=right))
    greet(at(y_=left))

    @pl.loop(1, nxz)
    def _(k):
        greet(plane(k))

    @pl.loop(0, nx)
    def _(k):
        greet(at(x_=lax.rem(x + k, nx), c_=1 - c))

    loads = []
    for ch in range(CH):
        loads.append(pltpu.make_async_copy(
            trials.at[pl.ds(ch * rc, rc)], xg.at[0, ch, 0], load_sem.at[ch]))
    gap_load = pltpu.make_async_copy(gaps, gapv, load_sem.at[2])
    nf = 4
    fr = pairs // nf
    f_loads = [pltpu.make_async_copy(
        factor.at[pl.ds(i * fr, fr)], f32v.at[pl.ds(i * fr, fr)], load_sem.at[4 + i])
        for i in range(nf)]
    s_load = pltpu.make_async_copy(stored, s32v, load_sem.at[3])
    for d in loads + [gap_load] + f_loads + [s_load]:
        d.start()
    for d in loads:
        d.wait()
    pl.semaphore_wait(bar, 2 + (nxz - 1) + nx)

    started = []

    def go(d):
        d.start()
        started.append(d)

    def ag_start(r, ch):
        own = xg.at[r, ch, 0]
        for i in range(2):
            lo, hi = pl.ds(i * rh, rh), pl.ds((1 - i) * rh, rh)
            go(remote(own.at[lo], xg.at[r, ch, 1, lo], ag_s.at[r, ch, i], ag_r.at[r, ch, i],
                      at(y_=right)))
            go(remote(own.at[hi], xg.at[r, ch, 2, hi], ag_s.at[r, ch, 3 - i],
                      ag_r.at[r, ch, 3 - i], at(y_=left)))

    def ag_landed(r, ch, slot, i, sem):
        part = xg.at[r, ch, slot, pl.ds(i * rh, rh)]
        remote(part, part, ag_s.at[r, ch, sem], ag_r.at[r, ch, sem], at(y_=right)).wait_recv()

    def ag_relay(r, ch):
        ag_landed(r, ch, 1, 0, 0)
        a = pl.ds(0, rh)
        go(remote(xg.at[r, ch, 1, a], xg.at[r, ch, 3, a], ag_s.at[r, ch, 4], ag_r.at[r, ch, 4],
                  at(y_=right)))
        ag_landed(r, ch, 2, 1, 3)
        b = pl.ds(rh, rh)
        go(remote(xg.at[r, ch, 2, b], xg.at[r, ch, 3, b], ag_s.at[r, ch, 5], ag_r.at[r, ch, 5],
                  at(y_=left)))

    def ag_finish(r, ch):
        ag_landed(r, ch, 1, 1, 1)
        ag_landed(r, ch, 2, 0, 2)
        ag_landed(r, ch, 3, 0, 4)
        ag_landed(r, ch, 3, 1, 5)

    def fitted_partial(r, ch):
        for s in range(4):
            hi, lo = halves(xg[r, ch, s])
            xs[pl.ds(s * rc, rc)] = hi
            xs[pl.ds(m + s * rc, rc)] = lo
        tn = min(256, aux)

        @pl.loop(0, aux // tn)
        def _(n):
            cols = pl.ds(pl.multiple_of(n * tn, tn), tn)
            fp[r, ch, :, cols] = dot3(xs[...], m, fhi[:, cols], flo[:, cols], NN)

    def ar_core(r, ch):
        mine = pl.ds(pl.multiple_of((1 - c) * half, half), half)
        go(remote(fp.at[r, ch, mine], fx.at[r, ch], cx_s.at[r, ch], cx_r.at[r, ch],
                  at(c_=1 - c)))

    def ar_scatter(r, ch):
        remote(fx.at[r, ch], fx.at[r, ch], cx_s.at[r, ch], cx_r.at[r, ch],
               at(c_=1 - c)).wait_recv()
        own = pl.ds(pl.multiple_of(c * half, half), half)
        fsum[r, ch] = fp[r, ch, own, :] + fx[r, ch]

        @pl.loop(1, nxz)
        def _(k):
            to = plane(k)
            src = fsum.at[r, ch, pl.ds(pl.multiple_of(to[0] * rb, rb), rb),
                          pl.ds(pl.multiple_of(to[1] * cb, cb), cb)]
            remote(src, rbuf.at[r, ch, k], pr_s.at[r, ch], pr_r.at[r, ch], to).start()

    def ar_gather(r, ch):
        arrived(rbuf.at[r, ch, pl.ds(1, nxz - 1)], pr_r.at[r, ch])
        total = fsum[r, ch, pl.ds(pl.multiple_of(x * rb, rb), rb),
                     pl.ds(pl.multiple_of(z * cb, cb), cb)]
        total = lax.fori_loop(1, nxz, lambda k, t: t + rbuf[r, ch, k], total)
        piece[r, ch] = total
        here = (pl.ds(pl.multiple_of(c * half + x * rb, rb), rb),
                pl.ds(pl.multiple_of(z * cb, cb), cb))
        fit[r, ch, here[0], here[1]] = total

        @pl.loop(1, nxz)
        def _(k):
            remote(piece.at[r, ch], fit.at[r, ch, here[0], here[1]], pa_s.at[r, ch],
                   pa_r.at[r, ch], plane(k)).start()

    def ar_swap(r, ch):
        arrived(rbuf.at[r, ch, pl.ds(1, nxz - 1)], pa_r.at[r, ch])
        own = fit.at[r, ch, pl.ds(pl.multiple_of(c * half, half), half)]
        go(remote(own, own, cy_s.at[r, ch], cy_r.at[r, ch], at(c_=1 - c)))

    def ar_finish(r, ch):
        other = fit.at[r, ch, pl.ds(pl.multiple_of((1 - c) * half, half), half)]
        remote(other, other, cy_s.at[r, ch], cy_r.at[r, ch], at(c_=1 - c)).wait_recv()

    def spread(r, ch):
        hi, lo = halves(fit[r, ch])
        fs[pl.ds(0, m)] = hi
        fs[pl.ds(m, m)] = lo
        tn = min(256, pairs)

        @pl.loop(0, pairs // tn)
        def _(n):
            cols = pl.ds(pl.multiple_of(n * tn, tn), tn)
            v = dot3(fs[...], m, fhi[cols, :], flo[cols, :], NT)
            for s in range(4):
                w[r, ch, s, :, cols] = v[s * rc:(s + 1) * rc]

    def rs_start(r, ch):
        a, b = pl.ds(0, rh), pl.ds(rh, rh)
        go(remote(w.at[r, ch, 3, a], tbuf.at[r, ch, 0], ys_s.at[r, ch, 0], ys_r.at[r, ch, 0],
                  at(y_=right)))
        go(remote(w.at[r, ch, 3, b], tbuf.at[r, ch, 1], ys_s.at[r, ch, 1], ys_r.at[r, ch, 1],
                  at(y_=left)))
        go(remote(w.at[r, ch, 2, b], win.at[r, ch, 0, b], ys_s.at[r, ch, 2], ys_r.at[r, ch, 2],
                  at(y_=right)))
        go(remote(w.at[r, ch, 1, a], win.at[r, ch, 1, a], ys_s.at[r, ch, 3], ys_r.at[r, ch, 3],
                  at(y_=left)))

    def rs_relay(r, ch):
        a, b = pl.ds(0, rh), pl.ds(rh, rh)
        remote(tbuf.at[r, ch, 0], tbuf.at[r, ch, 0], ys_s.at[r, ch, 0], ys_r.at[r, ch, 0],
               at(y_=right)).wait_recv()
        tbuf[r, ch, 0] = tbuf[r, ch, 0] + w[r, ch, 2, a]
        go(remote(tbuf.at[r, ch, 0], win.at[r, ch, 0, a], ys_s.at[r, ch, 4], ys_r.at[r, ch, 4],
                  at(y_=right)))
        remote(tbuf.at[r, ch, 1], tbuf.at[r, ch, 1], ys_s.at[r, ch, 1], ys_r.at[r, ch, 1],
               at(y_=left)).wait_recv()
        tbuf[r, ch, 1] = tbuf[r, ch, 1] + w[r, ch, 1, b]
        go(remote(tbuf.at[r, ch, 1], win.at[r, ch, 1, b], ys_s.at[r, ch, 5], ys_r.at[r, ch, 5],
                  at(y_=left)))

    def rs_finish(r, ch, inv):
        a, b = pl.ds(0, rh), pl.ds(rh, rh)
        for side, part, sem in ((0, b, 2), (1, a, 3), (0, a, 4), (1, b, 5)):
            ref = win.at[r, ch, side, part]
            remote(ref, ref, ys_s.at[r, ch, sem], ys_r.at[r, ch, sem], at(y_=right)).wait_recv()
        value = gapv[...] * xg[r, ch, 0] + 4.0 * (w[r, ch, 0] + win[r, ch, 0] + win[r, ch, 1])
        if inv is not None:
            value = value * inv[ch * rc:(ch + 1) * rc]
        resp[pl.ds(ch * rc, rc)] = value
        hi, lo = halves(value)
        rs[pl.ds(0, rc)] = hi
        rs[pl.ds(rc, rc)] = lo
        pp[r, pl.ds(ch * rc, rc)] = dot3(rs[...], rc, shi[...], slo[...], NT)

    def proj_start(r):
        @pl.loop(1, nxc)
        def _(k):
            to = row_peer(k)
            src = pp.at[r, pl.ds(pl.multiple_of((to[0] * 2 + to[2]) * pr, pr), pr)]
            remote(src, prx.at[r, k], px_s.at[r], px_r.at[r], to).start()

        arrived(prx.at[r, pl.ds(1, nxc - 1)], px_r.at[r])
        mine = pl.ds(pl.multiple_of((x * 2 + c) * pr, pr), pr)
        total = lax.fori_loop(1, nxc, lambda k, t: t + prx[r, k], pp[r, mine, :])
        psm[r] = total
        prz[r, z] = total

        @pl.loop(1, nz)
        def _(k):
            remote(psm.at[r], prz.at[r, z], pz_s.at[r], pz_r.at[r], z_peer(k)).start()

    def proj_finish(r):
        arrived(prz.at[r, pl.ds(1, nz - 1)], pz_r.at[r])
        mine = pl.ds(pl.multiple_of((x * 2 + c) * pr, pr), pr)
        total = lax.fori_loop(1, nz, lambda k, t: t + prz[r, k], prz[r, 0])
        pz[r] = total
        pfull[r, mine, :] = total

        @pl.loop(1, nxc)
        def _(k):
            remote(pz.at[r], pfull.at[r, mine], py_s.at[r], py_r.at[r], row_peer(k)).start()

        arrived(prx.at[r, pl.ds(1, nxc - 1)], py_r.at[r])
        o_proj[r] = pfull[r]

    def removed(r, ch, dest):
        hi, lo = halves(pfull[r, pl.ds(ch * rc, rc)])
        p2 = jnp.concatenate([hi, lo], axis=0)
        tn = min(256, pairs)

        def step(n, acc):
            cols = pl.ds(pl.multiple_of(n * tn, tn), tn)
            v = dot3(p2, rc, shi[:, cols], slo[:, cols], NN)
            sc = (resp[pl.ds(ch * rc, rc), cols] - v) / gapv[:, cols]
            dest[:, cols] = sc
            return acc + jnp.sum(sc * sc, axis=1, keepdims=True)

        return lax.fori_loop(0, pairs // tn, step, jnp.zeros((rc, 1), F32))

    def squares_start(r, sums):
        lane = lax.broadcasted_iota(jnp.int32, (8, 128), 1)
        t = jnp.zeros((8, 128), F32)
        for g in range(rows // 8):
            t = jnp.where(lane == g, sums[8 * g:8 * g + 8], t)
        sq0[r] = t

        @pl.loop(1, nxc)
        def _(k):
            remote(sq0.at[r], srx.at[r, k], qx_s.at[r], qx_r.at[r], row_peer(k)).start()

    def squares_middle(r):
        arrived(srx.at[r, pl.ds(1, nxc - 1)], qx_r.at[r])
        sq1[r] = lax.fori_loop(1, nxc, lambda k, t: t + srx[r, k], sq0[r])

        @pl.loop(1, nz)
        def _(k):
            remote(sq1.at[r], srz.at[r, k], qz_s.at[r], qz_r.at[r], z_peer(k)).start()

    def inverse_norms(r):
        arrived(srz.at[r, pl.ds(1, nz - 1)], qz_r.at[r])
        t = lax.fori_loop(1, nz, lambda k, t: t + srz[r, k], sq1[r])
        inv = 1.0 / jnp.sqrt(t / total_pairs + 1e-06)
        return jnp.concatenate([inv[:, g:g + 1] for g in range(rows // 8)], axis=0)

    A, B = 0, 1
    inv = None
    for r in range(ROUNDS):
        if r == 0:
            ag_start(r, A)
            ag_relay(r, A)
            ag_start(r, B)
            gap_load.wait()
            for i, d in enumerate(f_loads):
                d.wait()
                tr = min(64, fr)

                @pl.loop(0, fr // tr)
                def _(t, i=i):
                    part = pl.ds(pl.multiple_of(i * fr + t * tr, tr), tr)
                    hi, lo = halves(f32v[part, :])
                    fhi[part, :] = hi
                    flo[part, :] = lo
        else:
            ag_relay(r, A)
        ag_finish(r, A)
        fitted_partial(r, A)
        ar_core(r, A)
        ag_relay(r, B)
        if r == 0:
            s_load.wait()
            ts = min(32, n_st)

            @pl.loop(0, n_st // ts)
            def _(t):
                part = pl.ds(pl.multiple_of(t * ts, ts), ts)
                hi, lo = halves(s32v[part, :])
                shi[part, :] = hi
                slo[part, :] = lo
        else:
            squares_middle(0)
        ar_scatter(r, A)
        ag_finish(r, B)
        fitted_partial(r, B)
        ar_core(r, B)
        ar_gather(r, A)
        ar_scatter(r, B)
        if r > 0:
            inv = inverse_norms(0)
        ar_swap(r, A)
        ar_gather(r, B)
        ar_finish(r, A)
        spread(r, A)
        rs_start(r, A)
        ar_swap(r, B)
        rs_relay(r, A)
        ar_finish(r, B)
        spread(r, B)
        rs_start(r, B)
        rs_finish(r, A, inv)
        rs_relay(r, B)
        rs_finish(r, B, inv)
        proj_start(r)
        proj_finish(r)
        if r + 1 < ROUNDS:
            sums = []
            for ch in range(CH):
                sums.append(removed(r, ch, xg.at[r + 1, ch, 0]))
                ag_start(r + 1, ch)
            squares_start(r, jnp.concatenate(sums, axis=0))
        else:
            sums = [removed(r, ch, o_next.at[pl.ds(ch * rc, rc)]) for ch in range(CH)]
            squares_start(r, jnp.concatenate(sums, axis=0))
            squares_middle(r)
            last = inverse_norms(r)
            o_next[...] = o_next[...] * last

    for d in started:
        d.wait_send()
    for r in range(ROUNDS):
        for ch in range(CH):
            arrived(rbuf.at[r, ch, pl.ds(1, nxz - 1)], pr_s.at[r, ch])
            arrived(rbuf.at[r, ch, pl.ds(1, nxz - 1)], pa_s.at[r, ch])
        arrived(prx.at[r, pl.ds(1, nxc - 1)], px_s.at[r])
        arrived(prz.at[r, pl.ds(1, nz - 1)], pz_s.at[r])
        arrived(prx.at[r, pl.ds(1, nxc - 1)], py_s.at[r])
        arrived(srx.at[r, pl.ds(1, nxc - 1)], qx_s.at[r])
        arrived(srz.at[r, pl.ds(1, nz - 1)], qz_s.at[r])


def on_device(nx, nz, total_pairs, factor, trials, stored, gaps):
    pairs, aux = factor.shape
    rows = trials.shape[0]
    n_st = stored.shape[0]
    rc = rows // CH
    m, half = 4 * rc, 2 * rc
    rb, cb = half // nx, aux // nz
    nxc = 2 * nx
    pr = rows // nxc
    V = pltpu.VMEM
    D = pltpu.SemaphoreType.DMA
    scratch = [
        V((pairs, aux), F32), V((pairs, aux), BF16), V((pairs, aux), BF16),
        V((n_st, pairs), F32), V((n_st, pairs), BF16), V((n_st, pairs), BF16),
        V((1, pairs), F32),
        V((ROUNDS, CH, 4, rc, pairs), F32),
        V((2 * m, pairs), BF16),
        V((ROUNDS, CH, m, aux), F32),
        V((ROUNDS, CH, half, aux), F32),
        V((ROUNDS, CH, half, aux), F32),
        V((ROUNDS, CH, nx * nz, rb, cb), F32),
        V((ROUNDS, CH, rb, cb), F32),
        V((ROUNDS, CH, m, aux), F32),
        V((2 * m, aux), BF16),
        V((ROUNDS, CH, 4, rc, pairs), F32),
        V((ROUNDS, CH, 2, rc // 2, pairs), F32),
        V((ROUNDS, CH, 2, rc, pairs), F32),
        V((rows, pairs), F32),
        V((2 * rc, pairs), BF16),
        V((ROUNDS, rows, n_st), F32),
        V((ROUNDS, nxc, pr, n_st), F32),
        V((ROUNDS, pr, n_st), F32),
        V((ROUNDS, nz, pr, n_st), F32),
        V((ROUNDS, pr, n_st), F32),
        V((ROUNDS, rows, n_st), F32),
        V((ROUNDS, nxc, 8, 128), F32),
        V((ROUNDS, 8, 128), F32),
        V((ROUNDS, nz, 8, 128), F32),
        V((ROUNDS, 8, 128), F32),
        D((8,)), D((ROUNDS, CH, 6)), D((ROUNDS, CH, 6)),
        D((ROUNDS, CH)), D((ROUNDS, CH)), D((ROUNDS, CH)), D((ROUNDS, CH)),
        D((ROUNDS, CH)), D((ROUNDS, CH)), D((ROUNDS, CH)), D((ROUNDS, CH)),
        D((ROUNDS, CH, 6)), D((ROUNDS, CH, 6)),
        D((ROUNDS,)), D((ROUNDS,)), D((ROUNDS,)), D((ROUNDS,)), D((ROUNDS,)), D((ROUNDS,)),
        D((ROUNDS,)), D((ROUNDS,)), D((ROUNDS,)), D((ROUNDS,)),
    ]
    any_spec = pl.BlockSpec(memory_space=pl.ANY)
    vmem_spec = pl.BlockSpec(memory_space=pltpu.VMEM)
    nxt, proj = pl.pallas_call(
        functools.partial(kernel, nx, nz, total_pairs),
        out_shape=(jax.ShapeDtypeStruct((rows, pairs), F32),
                   jax.ShapeDtypeStruct((ROUNDS, rows, n_st), F32)),
        in_specs=[any_spec] * 4,
        out_specs=(vmem_spec, vmem_spec),
        scratch_shapes=scratch,
        compiler_params=pltpu.CompilerParams(
            collective_id=0, has_side_effects=True, vmem_limit_bytes=66_000_000),
        name="response_rounds",
    )(factor, trials, stored, gaps.reshape(1, pairs))
    return nxt, jnp.swapaxes(proj, 1, 2)


def solution(mesh):
    nx, nz = 4, 8
    split = Mesh(
        mesh.devices.reshape(nx, nz, 2, mesh.shape["aux"]), ("x", "z", "core", "aux")
    )
    pair = ("x", "z", "core")
    return jax.shard_map(
        functools.partial(on_device, nx, nz, PAIRS),
        mesh=split,
        in_specs=(P(pair, "aux"), P("aux", pair), P(None, pair), P(pair)),
        out_specs=(P("aux", pair), P(None, None, "aux")),
        check_vma=False,
    )
```

time: 476 us -> 200 us (0.42); the launches traced: 467 us -> 199 us
  blocking collectives: 240 us -> 0 us
  Pallas kernels: 0 us -> 195 us
  waiting for transfers between devices: 82.9 us -> 0 us
  matrix products: 59 us -> 0 us
  local copies, waits for them, and re-layouts: 36.4 us -> 3.49 us
  other arithmetic: 23.8 us -> 0 us
  between operations: 14.7 us -> 0.64 us
  starting transfers between devices: 9.74 us -> 0 us
    all_to_all x14 -> x0, blocking collectives: 240 us -> none  [the longest x6 105 us: sum_at_owner(): lax.all_to_all(blocks, axis, split_axis=0, concat_axis=0, tiled=True)]
    pallas_call x0 -> x1, Pallas kernels: none -> 195 us  [on_device(): pl.pallas_call(functools.partial(kernel, nx, nz, total_pairs), out_shape=...]
    all_gather x2 -> x0, waiting for transfers between devices: 65.8 us -> none  [side_by_side(): whole = lax.all_gather(both, axis, axis=dim, tiled=True)]
    dot_general x8 -> x0, matrix products: 59 us -> none  [the longest x2 22.3 us: on_device(): jnp.dot(everything, factor, precision=highest, preferred_element_type=jnp...]
    all_to_all x2 -> x0, waiting for transfers between devices: 17.1 us -> none  [sent_to_all(): lax.all_to_all(jnp.broadcast_to(x[None], (count, *x.shape)), axis, 0, 0,...]
    another operation x8 -> x0, local copies, waits for them, and re-layouts: 14.3 us -> none  [the longest x4 7.63 us: split_up(): return jnp.moveaxis(x.reshape(*before, count, -1, *after), dim, 0)]
    reduce_sum x10 -> x0, other arithmetic: 14.2 us -> none  [the longest x6 11.1 us: sum_at_owner(): return arrived.sum(axis=0)]
    all_to_all x2 -> x0, starting transfers between devices: 9.66 us -> none  [sent_to_all(): lax.all_to_all(jnp.broadcast_to(x[None], (count, *x.shape)), axis, 0, 0,...]
  transfers between devices with their start and end apart: 4 -> 0, of which waited for: 4 -> 0; matrix products, arithmetic and copies ran while one was open for 1% -> 0% of each run, Pallas kernels for 0% -> 0%
where the time goes in v1:
time: 200 us; the launch traced here: 199 us
  Pallas kernels  195 us (98%)
  local copies, waits for them, and re-layouts  3.49 us (2%)
    pallas_call x1, Pallas kernels, on_device(): pl.pallas_call(functools.partial(kernel, nx, nz, total_pairs), out_shape=...  195 us

profile of v1, /device:TPU:1, one launch (start us, length us, event | category | flops | bytes accessed | tf_op | source)
XLA Modules:
  0.0 199.5 jit_solution(2377330750316591651)
XLA Ops:
  0.6 195.4 %response_rounds.1 = (f32[64,2048]{1,0:T(8,128)}, f32[2,64,384]{2,1,0:T(8,128)}) custom-call(f32[2048,1024]{1,0:T(8,128)} %factor.1, f32[64,2048]{1,0:T(8,128)} %trials.1, f32[384,2048]{1,0:T(8,128)} %stored.1, f32[1,2048]{1,0:T(1,128)} %bitcast.3), custom_call_target="tpu_custom_call" | custom-call | tf_op jit(solution)/shard_map/response_rounds/pallas_call | solution.py:455
  196.0 1.9 copy.8
  197.9 1.6 copy.9

commit v2 on v1

--- a/solution.py
+++ b/solution.py
@@ -10,12 +10,44 @@
 
 PAIRS = 131072
 ROUNDS = 2
-CH = 2
+CH = 4
+GR = 2
+PER = CH // GR
 MESH = pl.DeviceIdType.MESH
 F32 = jnp.float32
 BF16 = jnp.bfloat16
 NT = (((1,), (1,)), ((), ()))
 NN = (((1,), (0,)), ((), ()))
+(
+    FACTOR, TURN, STORED, SEND, RELAY, FIT, FIT_B, SCATTER, GATHER, SWAP, SPREAD, SPREAD_B,
+    PASS, RESPOND, MEET, MEET_Z, MEET_ALL, REMOVE, SQUARES, SQUARES_Z, NORMS,
+) = range(21)
+ORDER = (
+    (SEND, 0, 0), (RELAY, 0, 0), (FACTOR, 0, 1), (FACTOR, 0, 0), (SEND, 0, 1),
+    (FACTOR, 0, 2), (TURN, 0, 2), (FACTOR, 0, 3), (FIT, 0, 0), (RELAY, 0, 1), (SEND, 0, 2),
+    (FIT_B, 0, 0), (TURN, 0, 3), (SCATTER, 0, 0), (TURN, 0, 5), (FIT, 0, 1), (FIT_B, 0, 1),
+    (SCATTER, 0, 1), (RELAY, 0, 2), (TURN, 0, 4), (SEND, 0, 3), (TURN, 0, 6), (TURN, 0, 1),
+    (GATHER, 0, 0), (TURN, 0, 7), (TURN, 0, 0), (RELAY, 0, 3), (FIT, 0, 2), (GATHER, 0, 1),
+    (FIT_B, 0, 2), (SCATTER, 0, 2), (FIT, 0, 3), (SWAP, 0, 0), (FIT_B, 0, 3),
+    (SPREAD, 0, 0), (SPREAD_B, 0, 0), (SCATTER, 0, 3), (SWAP, 0, 1), (SPREAD, 0, 1),
+    (SPREAD_B, 0, 1), (GATHER, 0, 2), (PASS, 0, 0), (PASS, 0, 1), (STORED, 0, 0),
+    (GATHER, 0, 3), (RESPOND, 0, 0), (RESPOND, 0, 1), (MEET, 0, 0), (SWAP, 0, 2),
+    (SPREAD, 0, 2), (SPREAD_B, 0, 2), (MEET_Z, 0, 0), (SWAP, 0, 3), (SPREAD, 0, 3),
+    (SPREAD_B, 0, 3), (PASS, 0, 2), (MEET_ALL, 0, 0), (PASS, 0, 3), (REMOVE, 0, 0),
+    (SEND, 1, 0), (RESPOND, 0, 2), (RESPOND, 0, 3), (MEET, 0, 1), (RELAY, 1, 0),
+    (SEND, 1, 1), (MEET_Z, 0, 1), (FIT, 1, 0), (RELAY, 1, 1), (FIT_B, 1, 0),
+    (MEET_ALL, 0, 1), (SCATTER, 1, 0), (FIT, 1, 1), (FIT_B, 1, 1), (REMOVE, 0, 1),
+    (SEND, 1, 2), (SCATTER, 1, 1), (SQUARES, 0, 0), (RELAY, 1, 2), (SEND, 1, 3),
+    (SQUARES_Z, 0, 0), (GATHER, 1, 0), (GATHER, 1, 1), (RELAY, 1, 3), (FIT, 1, 2),
+    (FIT_B, 1, 2), (SCATTER, 1, 2), (NORMS, 0, 0), (SWAP, 1, 0), (FIT, 1, 3), (FIT_B, 1, 3),
+    (SCATTER, 1, 3), (SPREAD, 1, 0), (SWAP, 1, 1), (SPREAD_B, 1, 0), (GATHER, 1, 2),
+    (SPREAD, 1, 1), (SPREAD_B, 1, 1), (PASS, 1, 0), (GATHER, 1, 3), (PASS, 1, 1),
+    (SWAP, 1, 2), (SPREAD, 1, 2), (SPREAD_B, 1, 2), (SWAP, 1, 3), (SPREAD, 1, 3),
+    (SPREAD_B, 1, 3), (PASS, 1, 2), (RESPOND, 1, 0), (RESPOND, 1, 1), (MEET, 1, 0),
+    (PASS, 1, 3), (RESPOND, 1, 2), (RESPOND, 1, 3), (MEET, 1, 1), (MEET_Z, 1, 0),
+    (MEET_Z, 1, 1), (MEET_ALL, 1, 0), (MEET_ALL, 1, 1), (REMOVE, 1, 0), (REMOVE, 1, 1),
+    (SQUARES, 1, 0), (SQUARES_Z, 1, 0), (NORMS, 1, 0),
+)
 
 
 def halves(v):
@@ -34,9 +66,9 @@
 
 
 def kernel(nx, nz, total_pairs, factor, trials, stored, gaps, o_next, o_proj,
-           f32v, fhi, flo, s32v, shi, slo, gapv,
+           f32v, fhi, flo, fthi, ftlo, s32v, shi, slo, gapv,
            xg, xs, fp, fx, fsum, rbuf, piece, fit, fs, w, tbuf, win, resp, rs,
-           pp, prx, psm, prz, pz, pfull, srx, sq1, srz, sq0,
+           pp, prx, psm, prz, pz, pfull, srx, sq1, srz, sq0, invn, sums,
            load_sem, ag_s, ag_r, cx_s, cx_r, pr_s, pr_r, pa_s, pa_r, cy_s, cy_r,
            ys_s, ys_r, px_s, px_r, pz_s, pz_r, py_s, py_r, qx_s, qx_r, qz_s, qz_r):
     rows, pairs = trials.shape
@@ -50,7 +82,9 @@
     cb = aux // nz
     nxz = nx * nz
     nxc = 2 * nx
-    pr = rows // nxc
+    gr = rows // GR
+    pr = gr // nx
+    cw = pr_cols(n_st)
     x, z = lax.axis_index("x"), lax.axis_index("z")
     c, y = lax.axis_index("core"), lax.axis_index("aux")
     right, left = lax.rem(y + 1, 4), lax.rem(y + 3, 4)
@@ -96,13 +130,13 @@
     for ch in range(CH):
         loads.append(pltpu.make_async_copy(
             trials.at[pl.ds(ch * rc, rc)], xg.at[0, ch, 0], load_sem.at[ch]))
-    gap_load = pltpu.make_async_copy(gaps, gapv, load_sem.at[2])
+    gap_load = pltpu.make_async_copy(gaps, gapv, load_sem.at[CH])
     nf = 4
     fr = pairs // nf
     f_loads = [pltpu.make_async_copy(
-        factor.at[pl.ds(i * fr, fr)], f32v.at[pl.ds(i * fr, fr)], load_sem.at[4 + i])
+        factor.at[pl.ds(i * fr, fr)], f32v.at[pl.ds(i * fr, fr)], load_sem.at[CH + 2 + i])
         for i in range(nf)]
-    s_load = pltpu.make_async_copy(stored, s32v, load_sem.at[3])
+    s_load = pltpu.make_async_copy(stored, s32v, load_sem.at[CH + 1])
     for d in loads + [gap_load] + f_loads + [s_load]:
         d.start()
     for d in loads:
@@ -144,14 +178,16 @@
         ag_landed(r, ch, 3, 0, 4)
         ag_landed(r, ch, 3, 1, 5)
 
-    def fitted_partial(r, ch):
-        for s in range(4):
-            hi, lo = halves(xg[r, ch, s])
-            xs[pl.ds(s * rc, rc)] = hi
-            xs[pl.ds(m + s * rc, rc)] = lo
-        tn = min(256, aux)
-
-        @pl.loop(0, aux // tn)
+    def fitted_partial(r, ch, part):
+        if part == 0:
+            for s in range(4):
+                hi, lo = halves(xg[r, ch, s])
+                xs[pl.ds(s * rc, rc)] = hi
+                xs[pl.ds(m + s * rc, rc)] = lo
+        tn = min(512, aux // 2)
+        n_all = aux // tn
+
+        @pl.loop(part * n_all // 2, (part + 1) * n_all // 2)
         def _(n):
             cols = pl.ds(pl.multiple_of(n * tn, tn), tn)
             fp[r, ch, :, cols] = dot3(xs[...], m, fhi[:, cols], flo[:, cols], NN)
@@ -178,7 +214,8 @@
         arrived(rbuf.at[r, ch, pl.ds(1, nxz - 1)], pr_r.at[r, ch])
         total = fsum[r, ch, pl.ds(pl.multiple_of(x * rb, rb), rb),
                      pl.ds(pl.multiple_of(z * cb, cb), cb)]
-        total = lax.fori_loop(1, nxz, lambda k, t: t + rbuf[r, ch, k], total)
+        for k in range(1, nxz):
+            total = total + rbuf[r, ch, k]
         piece[r, ch] = total
         here = (pl.ds(pl.multiple_of(c * half + x * rb, rb), rb),
                 pl.ds(pl.multiple_of(z * cb, cb), cb))
@@ -198,16 +235,18 @@
         other = fit.at[r, ch, pl.ds(pl.multiple_of((1 - c) * half, half), half)]
         remote(other, other, cy_s.at[r, ch], cy_r.at[r, ch], at(c_=1 - c)).wait_recv()
 
-    def spread(r, ch):
-        hi, lo = halves(fit[r, ch])
-        fs[pl.ds(0, m)] = hi
-        fs[pl.ds(m, m)] = lo
-        tn = min(256, pairs)
-
-        @pl.loop(0, pairs // tn)
+    def spread(r, ch, part):
+        if part == 0:
+            hi, lo = halves(fit[r, ch])
+            fs[pl.ds(0, m)] = hi
+            fs[pl.ds(m, m)] = lo
+        tn = min(512, pairs // 2)
+        n_all = pairs // tn
+
+        @pl.loop(part * n_all // 2, (part + 1) * n_all // 2)
         def _(n):
             cols = pl.ds(pl.multiple_of(n * tn, tn), tn)
-            v = dot3(fs[...], m, fhi[cols, :], flo[cols, :], NT)
+            v = dot3(fs[...], m, fthi[:, cols], ftlo[:, cols], NN)
             for s in range(4):
                 w[r, ch, s, :, cols] = v[s * rc:(s + 1) * rc]
 
@@ -235,70 +274,90 @@
         go(remote(tbuf.at[r, ch, 1], win.at[r, ch, 1, b], ys_s.at[r, ch, 5], ys_r.at[r, ch, 5],
                   at(y_=left)))
 
-    def rs_finish(r, ch, inv):
+    def rs_finish(r, ch):
         a, b = pl.ds(0, rh), pl.ds(rh, rh)
         for side, part, sem in ((0, b, 2), (1, a, 3), (0, a, 4), (1, b, 5)):
             ref = win.at[r, ch, side, part]
             remote(ref, ref, ys_s.at[r, ch, sem], ys_r.at[r, ch, sem], at(y_=right)).wait_recv()
+        mine = pl.ds(ch * rc, rc)
         value = gapv[...] * xg[r, ch, 0] + 4.0 * (w[r, ch, 0] + win[r, ch, 0] + win[r, ch, 1])
-        if inv is not None:
-            value = value * inv[ch * rc:(ch + 1) * rc]
-        resp[pl.ds(ch * rc, rc)] = value
+        if r > 0:
+            value = value * invn[r - 1, mine, 0:1]
+        resp[mine] = value
         hi, lo = halves(value)
-        rs[pl.ds(0, rc)] = hi
-        rs[pl.ds(rc, rc)] = lo
-        pp[r, pl.ds(ch * rc, rc)] = dot3(rs[...], rc, shi[...], slo[...], NT)
-
-    def proj_start(r):
+        at_group = (ch % PER) * rc
+        rs[pl.ds(at_group, rc)] = hi
+        rs[pl.ds(gr + at_group, rc)] = lo
+
+    def proj_start(r, g):
+        pp[r, g, :, pl.ds(0, n_st)] = dot3(rs[...], gr, shi[...], slo[...], NT)
+        if 2 * cw > n_st:
+            pp[r, g, :, pl.ds(n_st, 2 * cw - n_st)] = jnp.zeros((gr, 2 * cw - n_st), F32)
+
         @pl.loop(1, nxc)
         def _(k):
             to = row_peer(k)
-            src = pp.at[r, pl.ds(pl.multiple_of((to[0] * 2 + to[2]) * pr, pr), pr)]
-            remote(src, prx.at[r, k], px_s.at[r], px_r.at[r], to).start()
-
-        arrived(prx.at[r, pl.ds(1, nxc - 1)], px_r.at[r])
-        mine = pl.ds(pl.multiple_of((x * 2 + c) * pr, pr), pr)
-        total = lax.fori_loop(1, nxc, lambda k, t: t + prx[r, k], pp[r, mine, :])
-        psm[r] = total
-        prz[r, z] = total
+            src = pp.at[r, g, pl.ds(pl.multiple_of(to[0] * pr, pr), pr),
+                        pl.ds(pl.multiple_of(to[2] * cw, cw), cw)]
+            remote(src, prx.at[r, g, k], px_s.at[r, g], px_r.at[r, g], to).start()
+
+    def proj_middle(r, g):
+        arrived(prx.at[r, g, pl.ds(1, nxc - 1)], px_r.at[r, g])
+        own = pp[r, g, pl.ds(pl.multiple_of(x * pr, pr), pr),
+                 pl.ds(pl.multiple_of(c * cw, cw), cw)]
+        for k in range(1, nxc):
+            own = own + prx[r, g, k]
+        psm[r, g] = own
+        prz[r, g, z] = own
 
         @pl.loop(1, nz)
         def _(k):
-            remote(psm.at[r], prz.at[r, z], pz_s.at[r], pz_r.at[r], z_peer(k)).start()
-
-    def proj_finish(r):
-        arrived(prz.at[r, pl.ds(1, nz - 1)], pz_r.at[r])
-        mine = pl.ds(pl.multiple_of((x * 2 + c) * pr, pr), pr)
-        total = lax.fori_loop(1, nz, lambda k, t: t + prz[r, k], prz[r, 0])
-        pz[r] = total
-        pfull[r, mine, :] = total
+            remote(psm.at[r, g], prz.at[r, g, z], pz_s.at[r, g], pz_r.at[r, g],
+                   z_peer(k)).start()
+
+    def proj_finish(r, g):
+        arrived(prz.at[r, g, pl.ds(1, nz - 1)], pz_r.at[r, g])
+        total = prz[r, g, 0]
+        for k in range(1, nz):
+            total = total + prz[r, g, k]
+        pz[r, g] = total
+        here = (pl.ds(pl.multiple_of(x * pr, pr), pr), pl.ds(pl.multiple_of(c * cw, cw), cw))
+        pfull[r, g, here[0], here[1]] = total
 
         @pl.loop(1, nxc)
         def _(k):
-            remote(pz.at[r], pfull.at[r, mine], py_s.at[r], py_r.at[r], row_peer(k)).start()
-
-        arrived(prx.at[r, pl.ds(1, nxc - 1)], py_r.at[r])
-        o_proj[r] = pfull[r]
-
-    def removed(r, ch, dest):
-        hi, lo = halves(pfull[r, pl.ds(ch * rc, rc)])
+            remote(pz.at[r, g], pfull.at[r, g, here[0], here[1]], py_s.at[r, g],
+                   py_r.at[r, g], row_peer(k)).start()
+
+    def proj_done(r, g):
+        arrived(prx.at[r, g, pl.ds(1, nxc - 1)], py_r.at[r, g])
+        o_proj[r, pl.ds(g * gr, gr)] = pfull[r, g, :, pl.ds(0, n_st)]
+
+    def removed(r, g):
+        mine = pl.ds(g * gr, gr)
+        hi, lo = halves(pfull[r, g, :, pl.ds(0, n_st)])
         p2 = jnp.concatenate([hi, lo], axis=0)
-        tn = min(256, pairs)
+        tn = min(512, pairs)
 
         def step(n, acc):
             cols = pl.ds(pl.multiple_of(n * tn, tn), tn)
-            v = dot3(p2, rc, shi[:, cols], slo[:, cols], NN)
-            sc = (resp[pl.ds(ch * rc, rc), cols] - v) / gapv[:, cols]
-            dest[:, cols] = sc
+            v = dot3(p2, gr, shi[:, cols], slo[:, cols], NN)
+            sc = (resp[mine, cols] - v) / gapv[:, cols]
+            if r + 1 < ROUNDS:
+                for i in range(PER):
+                    xg[r + 1, g * PER + i, 0, :, cols] = sc[i * rc:(i + 1) * rc]
+            else:
+                o_next[mine, cols] = sc
             return acc + jnp.sum(sc * sc, axis=1, keepdims=True)
 
-        return lax.fori_loop(0, pairs // tn, step, jnp.zeros((rc, 1), F32))
-
-    def squares_start(r, sums):
+        acc = lax.fori_loop(0, pairs // tn, step, jnp.zeros((gr, 1), F32))
+        sums[r, mine] = jnp.broadcast_to(acc, (gr, 128))
+
+    def squares_start(r):
         lane = lax.broadcasted_iota(jnp.int32, (8, 128), 1)
         t = jnp.zeros((8, 128), F32)
         for g in range(rows // 8):
-            t = jnp.where(lane == g, sums[8 * g:8 * g + 8], t)
+            t = jnp.where(lane == g, sums[r, pl.ds(8 * g, 8)], t)
         sq0[r] = t
 
         @pl.loop(1, nxc)
@@ -307,7 +366,10 @@
 
     def squares_middle(r):
         arrived(srx.at[r, pl.ds(1, nxc - 1)], qx_r.at[r])
-        sq1[r] = lax.fori_loop(1, nxc, lambda k, t: t + srx[r, k], sq0[r])
+        t = sq0[r]
+        for k in range(1, nxc):
+            t = t + srx[r, k]
+        sq1[r] = t
 
         @pl.loop(1, nz)
         def _(k):
@@ -315,81 +377,93 @@
 
     def inverse_norms(r):
         arrived(srz.at[r, pl.ds(1, nz - 1)], qz_r.at[r])
-        t = lax.fori_loop(1, nz, lambda k, t: t + srz[r, k], sq1[r])
+        t = sq1[r]
+        for k in range(1, nz):
+            t = t + srz[r, k]
         inv = 1.0 / jnp.sqrt(t / total_pairs + 1e-06)
-        return jnp.concatenate([inv[:, g:g + 1] for g in range(rows // 8)], axis=0)
-
-    A, B = 0, 1
-    inv = None
-    for r in range(ROUNDS):
-        if r == 0:
-            ag_start(r, A)
-            ag_relay(r, A)
-            ag_start(r, B)
+        for g in range(rows // 8):
+            invn[r, pl.ds(8 * g, 8)] = jnp.broadcast_to(inv[:, g:g + 1], (8, 128))
+
+    def split_factor(i):
+        if i == 0:
             gap_load.wait()
-            for i, d in enumerate(f_loads):
-                d.wait()
-                tr = min(64, fr)
-
-                @pl.loop(0, fr // tr)
-                def _(t, i=i):
-                    part = pl.ds(pl.multiple_of(i * fr + t * tr, tr), tr)
-                    hi, lo = halves(f32v[part, :])
-                    fhi[part, :] = hi
-                    flo[part, :] = lo
-        else:
-            ag_relay(r, A)
-        ag_finish(r, A)
-        fitted_partial(r, A)
-        ar_core(r, A)
-        ag_relay(r, B)
-        if r == 0:
-            s_load.wait()
-            ts = min(32, n_st)
-
-            @pl.loop(0, n_st // ts)
-            def _(t):
-                part = pl.ds(pl.multiple_of(t * ts, ts), ts)
-                hi, lo = halves(s32v[part, :])
-                shi[part, :] = hi
-                slo[part, :] = lo
-        else:
-            squares_middle(0)
-        ar_scatter(r, A)
-        ag_finish(r, B)
-        fitted_partial(r, B)
-        ar_core(r, B)
-        ar_gather(r, A)
-        ar_scatter(r, B)
-        if r > 0:
-            inv = inverse_norms(0)
-        ar_swap(r, A)
-        ar_gather(r, B)
-        ar_finish(r, A)
-        spread(r, A)
-        rs_start(r, A)
-        ar_swap(r, B)
-        rs_relay(r, A)
-        ar_finish(r, B)
-        spread(r, B)
-        rs_start(r, B)
-        rs_finish(r, A, inv)
-        rs_relay(r, B)
-        rs_finish(r, B, inv)
-        proj_start(r)
-        proj_finish(r)
-        if r + 1 < ROUNDS:
-            sums = []
-            for ch in range(CH):
-                sums.append(removed(r, ch, xg.at[r + 1, ch, 0]))
-                ag_start(r + 1, ch)
-            squares_start(r, jnp.concatenate(sums, axis=0))
-        else:
-            sums = [removed(r, ch, o_next.at[pl.ds(ch * rc, rc)]) for ch in range(CH)]
-            squares_start(r, jnp.concatenate(sums, axis=0))
-            squares_middle(r)
-            last = inverse_norms(r)
-            o_next[...] = o_next[...] * last
+        f_loads[i].wait()
+        tr = min(64, fr)
+
+        @pl.loop(0, fr // tr)
+        def _(t):
+            part = pl.ds(pl.multiple_of(i * fr + t * tr, tr), tr)
+            hi, lo = halves(f32v[part, :])
+            fhi[part, :] = hi
+            flo[part, :] = lo
+
+    def turn_factor(i):
+        tp, ta = pairs // 8, min(256, aux)
+
+        @pl.loop(0, aux // ta)
+        def _(n):
+            cols = pl.ds(pl.multiple_of(n * ta, ta), ta)
+            hi, lo = halves(f32v[pl.ds(i * tp, tp), cols].T)
+            fthi[cols, pl.ds(i * tp, tp)] = hi
+            ftlo[cols, pl.ds(i * tp, tp)] = lo
+
+    def split_stored():
+        s_load.wait()
+        ts = min(32, n_st)
+
+        @pl.loop(0, n_st // ts)
+        def _(t):
+            part = pl.ds(pl.multiple_of(t * ts, ts), ts)
+            hi, lo = halves(s32v[part, :])
+            shi[part, :] = hi
+            slo[part, :] = lo
+
+    def last_spread(r, ch):
+        spread(r, ch, 1)
+        rs_start(r, ch)
+
+    def last_fitted(r, ch):
+        fitted_partial(r, ch, 1)
+        ar_core(r, ch)
+
+    def first_spread(r, ch):
+        ar_finish(r, ch)
+        spread(r, ch, 0)
+
+    def first_fitted(r, ch):
+        ag_finish(r, ch)
+        fitted_partial(r, ch, 0)
+
+    def remainder(r, g):
+        proj_done(r, g)
+        removed(r, g)
+
+    stages = {
+        FACTOR: lambda _, i: split_factor(i),
+        TURN: lambda _, i: turn_factor(i),
+        STORED: lambda *_: split_stored(),
+        SEND: ag_start,
+        RELAY: ag_relay,
+        FIT: first_fitted,
+        FIT_B: last_fitted,
+        SCATTER: ar_scatter,
+        GATHER: ar_gather,
+        SWAP: ar_swap,
+        SPREAD: first_spread,
+        SPREAD_B: last_spread,
+        PASS: rs_relay,
+        RESPOND: rs_finish,
+        MEET: proj_start,
+        MEET_Z: proj_middle,
+        MEET_ALL: proj_finish,
+        REMOVE: remainder,
+        SQUARES: lambda r, _: squares_start(r),
+        SQUARES_Z: lambda r, _: squares_middle(r),
+        NORMS: lambda r, _: inverse_norms(r),
+    }
+    for stage, r, i in ORDER:
+        stages[stage](r, i)
+    o_next[...] = o_next[...] * invn[ROUNDS - 1, :, 0:1]
 
     for d in started:
         d.wait_send()
@@ -397,11 +471,16 @@
         for ch in range(CH):
             arrived(rbuf.at[r, ch, pl.ds(1, nxz - 1)], pr_s.at[r, ch])
             arrived(rbuf.at[r, ch, pl.ds(1, nxz - 1)], pa_s.at[r, ch])
-        arrived(prx.at[r, pl.ds(1, nxc - 1)], px_s.at[r])
-        arrived(prz.at[r, pl.ds(1, nz - 1)], pz_s.at[r])
-        arrived(prx.at[r, pl.ds(1, nxc - 1)], py_s.at[r])
+        for g in range(GR):
+            arrived(prx.at[r, g, pl.ds(1, nxc - 1)], px_s.at[r, g])
+            arrived(prz.at[r, g, pl.ds(1, nz - 1)], pz_s.at[r, g])
+            arrived(prx.at[r, g, pl.ds(1, nxc - 1)], py_s.at[r, g])
         arrived(srx.at[r, pl.ds(1, nxc - 1)], qx_s.at[r])
         arrived(srz.at[r, pl.ds(1, nz - 1)], qz_s.at[r])
+
+
+def pr_cols(n_st):
+    return -(-n_st // 256) * 128
 
 
 def on_device(nx, nz, total_pairs, factor, trials, stored, gaps):
@@ -412,11 +491,13 @@
     m, half = 4 * rc, 2 * rc
     rb, cb = half // nx, aux // nz
     nxc = 2 * nx
-    pr = rows // nxc
+    gr = rows // GR
+    pr, cw = gr // nx, pr_cols(n_st)
     V = pltpu.VMEM
     D = pltpu.SemaphoreType.DMA
     scratch = [
         V((pairs, aux), F32), V((pairs, aux), BF16), V((pairs, aux), BF16),
+        V((aux, pairs), BF16), V((aux, pairs), BF16),
         V((n_st, pairs), F32), V((n_st, pairs), BF16), V((n_st, pairs), BF16),
         V((1, pairs), F32),
         V((ROUNDS, CH, 4, rc, pairs), F32),
@@ -432,22 +513,25 @@
         V((ROUNDS, CH, 2, rc // 2, pairs), F32),
         V((ROUNDS, CH, 2, rc, pairs), F32),
         V((rows, pairs), F32),
-        V((2 * rc, pairs), BF16),
-        V((ROUNDS, rows, n_st), F32),
-        V((ROUNDS, nxc, pr, n_st), F32),
-        V((ROUNDS, pr, n_st), F32),
-        V((ROUNDS, nz, pr, n_st), F32),
-        V((ROUNDS, pr, n_st), F32),
-        V((ROUNDS, rows, n_st), F32),
+        V((2 * gr, pairs), BF16),
+        V((ROUNDS, GR, gr, 2 * cw), F32),
+        V((ROUNDS, GR, nxc, pr, cw), F32),
+        V((ROUNDS, GR, pr, cw), F32),
+        V((ROUNDS, GR, nz, pr, cw), F32),
+        V((ROUNDS, GR, pr, cw), F32),
+        V((ROUNDS, GR, gr, 2 * cw), F32),
         V((ROUNDS, nxc, 8, 128), F32),
         V((ROUNDS, 8, 128), F32),
         V((ROUNDS, nz, 8, 128), F32),
         V((ROUNDS, 8, 128), F32),
-        D((8,)), D((ROUNDS, CH, 6)), D((ROUNDS, CH, 6)),
+        V((ROUNDS, rows, 128), F32),
+        V((ROUNDS, rows, 128), F32),
+        D((CH + 6,)), D((ROUNDS, CH, 6)), D((ROUNDS, CH, 6)),
         D((ROUNDS, CH)), D((ROUNDS, CH)), D((ROUNDS, CH)), D((ROUNDS, CH)),
         D((ROUNDS, CH)), D((ROUNDS, CH)), D((ROUNDS, CH)), D((ROUNDS, CH)),
         D((ROUNDS, CH, 6)), D((ROUNDS, CH, 6)),
-        D((ROUNDS,)), D((ROUNDS,)), D((ROUNDS,)), D((ROUNDS,)), D((ROUNDS,)), D((ROUNDS,)),
+        D((ROUNDS, GR)), D((ROUNDS, GR)), D((ROUNDS, GR)), D((ROUNDS, GR)),
+        D((ROUNDS, GR)), D((ROUNDS, GR)),
         D((ROUNDS,)), D((ROUNDS,)), D((ROUNDS,)), D((ROUNDS,)),
     ]
     any_spec = pl.BlockSpec(memory_space=pl.ANY)

time: 200 us -> 157 us (0.79)
  Pallas kernels: 195 us -> 152 us
    pallas_call x1, Pallas kernels: 195 us -> 152 us  [on_device(): pl.pallas_call(functools.partial(kernel, nx, nz, total_pairs), out_shape=...]
where the time goes in v2:
time: 157 us; the launch traced here: 156 us
  Pallas kernels  152 us (97%)
  local copies, waits for them, and re-layouts  3.49 us (2%)
    pallas_call x1, Pallas kernels, on_device(): pl.pallas_call(functools.partial(kernel, nx, nz, total_pairs), out_shape=...  152 us
    unnamed x2, local copies, waits for them, and re-layouts  3.49 us

profile of v2, /device:TPU:1, one launch (start us, length us, event | category | flops | bytes accessed | tf_op | source)
XLA Modules:
  0.0 156.4 jit_solution(16436050288711063004)
XLA Ops:
  0.6 152.3 %response_rounds.1 = (f32[64,2048]{1,0:T(8,128)}, f32[2,64,384]{2,1,0:T(8,128)}) custom-call(f32[2048,1024]{1,0:T(8,128)} %factor.1, f32[64,2048]{1,0:T(8,128)} %trials.1, f32[384,2048]{1,0:T(8,128)} %stored.1, f32[1,2048]{1,0:T(1,128)} %bitcast.3), custom_call_target="tpu_custom_call" | custom-call | tf_op jit(solution)/shard_map/response_rounds/pallas_call | solution.py:539
  153.0 1.9 %copy.8 = f32[64,2048]{1,0:T(8,128)} copy(f32[64,2048]{1,0:T(8,128)} %get-tuple-element.8) | data formatting | bytes 1048576
  154.8 1.6 %copy.9 = f32[2,384,64]{1,2,0:T(8,128)} copy(f32[2,384,64]{1,2,0:T(8,128)} %bitcast.2) | data formatting | bytes 393216

commit v3 on v2

--- a/solution.py
+++ b/solution.py
@@ -93,6 +93,15 @@
         pick = lambda v, d: d if v is None else v
         return (pick(x_, x), pick(z_, z), pick(c_, c), pick(y_, y))
 
+    def far_first(i, n):
+        return n // 2 + (1 - 2 * (i % 2)) * ((i + 1) // 2)
+
+    def plane_order(i):
+        return far_first(i % nx, nx) * nz + far_first(i // nx, nz)
+
+    def row_order(i):
+        return far_first(i // 2, nx) * 2 + 1 - i % 2
+
     def plane(k):
         return at(x_=lax.rem(x + k // nz, nx), z_=lax.rem(z + k % nz, nz))
 
@@ -203,8 +212,9 @@
         own = pl.ds(pl.multiple_of(c * half, half), half)
         fsum[r, ch] = fp[r, ch, own, :] + fx[r, ch]
 
-        @pl.loop(1, nxz)
-        def _(k):
+        @pl.loop(0, nxz - 1)
+        def _(i):
+            k = plane_order(i)
             to = plane(k)
             src = fsum.at[r, ch, pl.ds(pl.multiple_of(to[0] * rb, rb), rb),
                           pl.ds(pl.multiple_of(to[1] * cb, cb), cb)]
@@ -221,8 +231,9 @@
                 pl.ds(pl.multiple_of(z * cb, cb), cb))
         fit[r, ch, here[0], here[1]] = total
 
-        @pl.loop(1, nxz)
-        def _(k):
+        @pl.loop(0, nxz - 1)
+        def _(i):
+            k = plane_order(i)
             remote(piece.at[r, ch], fit.at[r, ch, here[0], here[1]], pa_s.at[r, ch],
                    pa_r.at[r, ch], plane(k)).start()
 
@@ -294,8 +305,9 @@
         if 2 * cw > n_st:
             pp[r, g, :, pl.ds(n_st, 2 * cw - n_st)] = jnp.zeros((gr, 2 * cw - n_st), F32)
 
-        @pl.loop(1, nxc)
-        def _(k):
+        @pl.loop(0, nxc - 1)
+        def _(i):
+            k = row_order(i)
             to = row_peer(k)
             src = pp.at[r, g, pl.ds(pl.multiple_of(to[0] * pr, pr), pr),
                         pl.ds(pl.multiple_of(to[2] * cw, cw), cw)]
@@ -310,8 +322,9 @@
         psm[r, g] = own
         prz[r, g, z] = own
 
-        @pl.loop(1, nz)
-        def _(k):
+        @pl.loop(0, nz - 1)
+        def _(i):
+            k = far_first(i, nz)
             remote(psm.at[r, g], prz.at[r, g, z], pz_s.at[r, g], pz_r.at[r, g],
                    z_peer(k)).start()
 
@@ -324,8 +337,9 @@
         here = (pl.ds(pl.multiple_of(x * pr, pr), pr), pl.ds(pl.multiple_of(c * cw, cw), cw))
         pfull[r, g, here[0], here[1]] = total
 
-        @pl.loop(1, nxc)
-        def _(k):
+        @pl.loop(0, nxc - 1)
+        def _(i):
+            k = row_order(i)
             remote(pz.at[r, g], pfull.at[r, g, here[0], here[1]], py_s.at[r, g],
                    py_r.at[r, g], row_peer(k)).start()
 
@@ -360,8 +374,9 @@
             t = jnp.where(lane == g, sums[r, pl.ds(8 * g, 8)], t)
         sq0[r] = t
 
-        @pl.loop(1, nxc)
-        def _(k):
+        @pl.loop(0, nxc - 1)
+        def _(i):
+            k = row_order(i)
             remote(sq0.at[r], srx.at[r, k], qx_s.at[r], qx_r.at[r], row_peer(k)).start()
 
     def squares_middle(r):
@@ -371,8 +386,9 @@
             t = t + srx[r, k]
         sq1[r] = t
 
-        @pl.loop(1, nz)
-        def _(k):
+        @pl.loop(0, nz - 1)
+        def _(i):
+            k = far_first(i, nz)
             remote(sq1.at[r], srz.at[r, k], qz_s.at[r], qz_r.at[r], z_peer(k)).start()
 
     def inverse_norms(r):

time: 157 us -> 158 us (level)
  Pallas kernels: 152 us -> 154 us
where the time goes in v3:
time: 158 us
  Pallas kernels  154 us (97%)
  local copies, waits for them, and re-layouts  3.49 us (2%)
    pallas_call x1, Pallas kernels, on_device(): pl.pallas_call(functools.partial(kernel, nx, nz, total_pairs), out_shape=...  154 us
    unnamed x2, local copies, waits for them, and re-layouts  3.49 us

profile of v3, /device:TPU:1, one launch (start us, length us, event | category | flops | bytes accessed | tf_op | source)
XLA Modules:
  0.0 157.7 jit_solution(4885839025565175061)
XLA Ops:
  0.6 153.6 %response_rounds.1 = (f32[64,2048]{1,0:T(8,128)}, f32[2,64,384]{2,1,0:T(8,128)}) custom-call(f32[2048,1024]{1,0:T(8,128)} %factor.1, f32[64,2048]{1,0:T(8,128)} %trials.1, f32[384,2048]{1,0:T(8,128)} %stored.1, f32[1,2048]{1,0:T(1,128)} %bitcast.3), custom_call_target="tpu_custom_call" | custom-call | tf_op jit(solution)/shard_map/response_rounds/pallas_call | solution.py:555
  154.2 1.9 %copy.8 = f32[64,2048]{1,0:T(8,128)} copy(f32[64,2048]{1,0:T(8,128)} %get-tuple-element.8) | data formatting | bytes 1048576
  156.1 1.6 %copy.9 = f32[2,384,64]{1,2,0:T(8,128)} copy(f32[2,384,64]{1,2,0:T(8,128)} %bitcast.2) | data formatting | bytes 393216

commit v4 on v2

--- a/solution.py
+++ b/solution.py
@@ -337,7 +337,7 @@
         mine = pl.ds(g * gr, gr)
         hi, lo = halves(pfull[r, g, :, pl.ds(0, n_st)])
         p2 = jnp.concatenate([hi, lo], axis=0)
-        tn = min(512, pairs)
+        tn = min(1024, pairs)
 
         def step(n, acc):
             cols = pl.ds(pl.multiple_of(n * tn, tn), tn)

time: 157 us -> 156 us (level)
  no operation moved by 1% of the time
where the time goes in v4:
time: 156 us
  Pallas kernels  151 us (97%)
  local copies, waits for them, and re-layouts  3.49 us (2%)
    pallas_call x1, Pallas kernels, on_device(): pl.pallas_call(functools.partial(kernel, nx, nz, total_pairs), out_shape=...  151 us
    unnamed x2, local copies, waits for them, and re-layouts  3.49 us

profile of v4, /device:TPU:1, one launch (start us, length us, event | category | flops | bytes accessed | tf_op | source)
XLA Modules:
  0.0 155.6 jit_solution(1132879888757036648)
XLA Ops:
  0.6 151.4 %response_rounds.1 = (f32[64,2048]{1,0:T(8,128)}, f32[2,64,384]{2,1,0:T(8,128)}) custom-call(f32[2048,1024]{1,0:T(8,128)} %factor.1, f32[64,2048]{1,0:T(8,128)} %trials.1, f32[384,2048]{1,0:T(8,128)} %stored.1, f32[1,2048]{1,0:T(1,128)} %bitcast.3), custom_call_target="tpu_custom_call" | custom-call | tf_op jit(solution)/shard_map/response_rounds/pallas_call | solution.py:539
  152.1 1.9 %copy.8 = f32[64,2048]{1,0:T(8,128)} copy(f32[64,2048]{1,0:T(8,128)} %get-tuple-element.8) | data formatting | bytes 1048576
  153.9 1.6 %copy.9 = f32[2,384,64]{1,2,0:T(8,128)} copy(f32[2,384,64]{1,2,0:T(8,128)} %bitcast.2) | data formatting | bytes 393216
